TPU v7x, 512 devices: a whole 4x4x16 slice. The times are simulated.
512 devices in a mesh: ctx: 64 (over x, z), head: 8 (over y, core).
Axes of the slice: x: 4, y: 4, z: 16, core: 2. Of those that a mesh axis runs over, the one named last changes fastest.
Arguments:
- lin_query: bfloat16 [16384, 4096], P('ctx', 'head'), may hold values from -200 to 200
- lin_keys: bfloat16 [16384, 4096], P('ctx', 'head'), may hold values from -6 to 6
- lin_values: bfloat16 [16384, 4096], P('ctx', 'head'), may hold values from -6 to 6
- lin_grad: bfloat16 [16384, 4096], P('ctx', 'head'), may hold values from -6 to 6
- norm_gain: float32 [4096], P('head'), may hold values from 0.1 to 1.9
- log_decay: float32 [32, 16384], P('head'), may hold values from -1 to 0, as said below
- state_in: bfloat16 [64, 32, 128, 128], P('ctx', 'head'), may hold values from -96 to 96
- soft_query: bfloat16 [16384, 8192], P('ctx', 'head'), may hold values from -10 to 10
- soft_keys: bfloat16 [16384, 1024], P('ctx', 'head'), may hold values from -4 to 4
- soft_values: bfloat16 [16384, 1024], P('ctx', 'head'), may hold values from -6 to 6
- soft_grad: bfloat16 [16384, 8192], P('ctx', 'head'), may hold values from -6 to 6
- projections: bfloat16 [2, 4096, 1024], P(None, None, 'head'), may hold values from -0.125 to 0.125
- doc_lengths: int32 [32], replicated, may hold values from 1 to 768, 16384 in all
Outputs:
- lin_dq: bfloat16 [16384, 4096], P('ctx', 'head')
- lin_dk: bfloat16 [16384, 4096], P('ctx', 'head')
- lin_dv: bfloat16 [16384, 4096], P('ctx', 'head')
- soft_dq: bfloat16 [16384, 8192], P('ctx', 'head')
- soft_dk: bfloat16 [16384, 1024], P('ctx', 'head')
- soft_dv: bfloat16 [16384, 1024], P('ctx', 'head')
Inputs may be any that keep to these rules, and one draw needn't show every extreme that they name: `log_decay`: strictly negative. `doc_lengths`: positive lengths that add up to 16384; the largest is exactly 768.
All inputs are finite; a program needn't handle non-finite values.
Results may differ from a plain program's by a relative error of at most 0.011.
Values may be sent and summed in bfloat16 or wider, within the bound.
No kernel may reach another device: no remote copies, remote signals or barrier semaphores. Data moves between devices by JAX's collectives and lax.ppermute only.
A program may use at most 128 MiB of HBM per device.

v0:
```python
import jax
import jax.numpy as jnp
from jax import lax
from jax.sharding import PartitionSpec as P

DH = 128
Q_HEADS = 64
KV_HEADS = 8
LIGHTNING_HEADS = 32
SUB = 4
epsilon = 1e-06
precise = lax.Precision.HIGHEST


def passed_along(block, axis, distance):
    devices = range(lax.axis_size(axis))
    route = [(i - distance, i) for i in devices if i - distance in devices]
    return lax.ppermute(block, axis, route)


def document_of(positions, doc_lengths):
    doc_ends = jnp.cumsum(doc_lengths)
    return jnp.sum((doc_ends[None, :] <= positions[:, None]).astype(jnp.int32), axis=1)


def decay_weights(log_block):
    running = jnp.cumsum(log_block, axis=1)
    position = jnp.arange(log_block.shape[1], dtype=jnp.int32)
    before = position[:, None] >= position[None, :]
    log_gap = running[:, :, None] - running[:, None, :]
    weights = jnp.where(before[None], jnp.exp(jnp.minimum(log_gap, 0.0)), 0.0)
    return (running, weights)


def lightning_part(lin_query, lin_keys, lin_values, cotangent, norm_gain, log_decay, state_in):
    length = lin_query.shape[0]
    head_count = lin_query.shape[1] // DH
    device = lax.axis_index("ctx")
    chain = lax.axis_size("ctx")
    log_block = lax.dynamic_slice_in_dim(log_decay, device * length, length, 1)
    running, weights = decay_weights(log_block)
    query_blk = lin_query.reshape(length, head_count, DH)
    key_blk = lin_keys.reshape(length, head_count, DH)
    value_blk = lin_values.reshape(length, head_count, DH)
    grad_blk = cotangent.reshape(length, head_count, DH)
    state_blk = state_in[0]
    near_terms = (
        jnp.einsum("thd,shd->hts", query_blk, key_blk, preferred_element_type=jnp.float32) * weights
    ).astype(jnp.bfloat16)
    growth = jnp.exp(running).T[:, :, None]
    scaled = (query_blk.astype(jnp.float32) * growth).astype(jnp.bfloat16)
    inside = jnp.einsum("hts,shd->thd", near_terms, value_blk, preferred_element_type=jnp.float32)
    carried = jnp.einsum("thd,hde->the", scaled, state_blk, preferred_element_type=jnp.float32)
    lin_out = (inside + carried) / DH
    gated = norm_gain.reshape(head_count, DH)[None] * grad_blk
    squares, cross_term = lax.psum(
        (jnp.sum(lin_out * lin_out, axis=(1, 2)), jnp.sum(gated * lin_out, axis=(1, 2))), "head"
    )
    features = LIGHTNING_HEADS * DH
    spread = jnp.sqrt(squares / features + epsilon)
    out_grad = (
        gated / spread[:, None, None]
        - lin_out * (cross_term / (features * spread**3))[:, None, None]
    ).astype(jnp.bfloat16)
    far_terms = (
        jnp.einsum("the,she->hts", out_grad, value_blk, preferred_element_type=jnp.float32)
        * weights
    ).astype(jnp.bfloat16)
    grad_query = (
        jnp.einsum("hts,shd->thd", far_terms, key_blk, preferred_element_type=jnp.float32)
        + growth
        * jnp.einsum("the,hde->thd", out_grad, state_blk, preferred_element_type=jnp.float32)
    ) / DH
    summary = jnp.einsum(
        "thd,the->hde", scaled, out_grad, preferred_element_type=jnp.float32
    ).astype(jnp.bfloat16)
    own_total = running[:, -1]
    totals = jnp.sum(log_decay.reshape(head_count, chain, length), axis=2)
    starts = jnp.concatenate(
        [jnp.zeros((head_count, 1), jnp.float32), jnp.cumsum(totals, axis=1)], axis=1
    )
    anchor = lax.dynamic_slice_in_dim(starts, device + 1, 1, 1)
    block_in = lax.all_gather(summary[None], "ctx", axis=0, tiled=True)
    block_count = block_in.shape[0]
    block_index = jnp.arange(block_count, dtype=jnp.int32)
    log_level = lax.slice_in_dim(starts, 0, block_count, axis=1)
    factors = jnp.where(
        block_index[None, :] > device, jnp.exp(jnp.minimum(log_level - anchor, 0.0)), 0.0
    )
    after_state = jnp.einsum(
        "hn,nhde->hde", factors, block_in.astype(jnp.float32), precision=precise
    )
    after_low = after_state.astype(jnp.bfloat16)
    tail_decay = jnp.exp(own_total[:, None] - running).T[:, :, None]
    grad_key = (
        jnp.einsum("hst,shd->thd", far_terms, query_blk, preferred_element_type=jnp.float32)
        + tail_decay
        * jnp.einsum("the,hde->thd", value_blk, after_low, preferred_element_type=jnp.float32)
    ) / DH
    grad_value = (
        jnp.einsum("hst,she->the", near_terms, out_grad, preferred_element_type=jnp.float32)
        + tail_decay
        * jnp.einsum("thd,hde->the", key_blk, after_low, preferred_element_type=jnp.float32)
    ) / DH
    flat = (length, head_count * DH)
    return (
        grad_query.astype(jnp.bfloat16).reshape(flat),
        grad_key.astype(jnp.bfloat16).reshape(flat),
        grad_value.astype(jnp.bfloat16).reshape(flat),
    )


def softmax_head(query_heads, grad_heads, key_win, value_win, visible):
    head_count, length, features = query_heads.shape
    per_turn = min(head_count, max(1, 512 // length))
    turn_count = head_count // per_turn
    query_steps = query_heads.reshape(turn_count, per_turn * length, features)
    grad_steps = grad_heads.reshape(turn_count, per_turn * length, features)
    visible_rows = jnp.tile(visible, (per_turn, 1))
    score_scale = DH ** (-0.5)
    contract_last = (((1,), (1,)), ((), ()))
    contract_first = (((0,), (0,)), ((), ()))

    def one_turn(running_sums, pieces):
        query_rows, grad_rows = pieces
        scores = (
            lax.dot_general(query_rows, key_win, contract_last, preferred_element_type=jnp.float32)
            * score_scale
        )
        scores = jnp.where(visible_rows, scores, -1e30)
        highest = jnp.max(scores, axis=1, keepdims=True)
        raised = jnp.where(visible_rows, jnp.exp(scores - highest), 0.0)
        attention = raised / jnp.sum(raised, axis=1, keepdims=True)
        prob_low = attention.astype(jnp.bfloat16)
        output = jnp.dot(prob_low, value_win, preferred_element_type=jnp.float32)
        row_delta = jnp.sum(grad_rows.astype(jnp.float32) * output, axis=1, keepdims=True)
        grad_probs = lax.dot_general(
            grad_rows, value_win, contract_last, preferred_element_type=jnp.float32
        )
        dscore = (attention * (grad_probs - row_delta) * score_scale).astype(jnp.bfloat16)
        grad_query = jnp.dot(dscore, key_win, preferred_element_type=jnp.float32).astype(
            jnp.bfloat16
        )
        part_key = lax.dot_general(
            dscore, query_rows, contract_first, preferred_element_type=jnp.float32
        )
        part_value = lax.dot_general(
            prob_low, grad_rows, contract_first, preferred_element_type=jnp.float32
        )
        return ((running_sums[0] + part_key, running_sums[1] + part_value), grad_query)

    zero_rows = jnp.zeros((key_win.shape[0], features), jnp.float32)
    sums_out, grad_query = lax.scan(one_turn, (zero_rows, zero_rows), (query_steps, grad_steps))
    return (sums_out[0], sums_out[1], grad_query.reshape(head_count, length, features))


def softmax_part(soft_query, soft_keys, soft_values, soft_grad, doc_lengths):
    length = soft_query.shape[0]
    kv_local = soft_keys.shape[1] // DH
    group_size = Q_HEADS // KV_HEADS
    device = lax.axis_index("ctx")
    stacked = jnp.stack([soft_keys, soft_values])
    arrived = [stacked] + [passed_along(stacked, "ctx", offset) for offset in range(1, SUB)]
    window = jnp.concatenate(arrived[::-1], axis=1)
    query_pos = device * length + jnp.arange(length, dtype=jnp.int32)
    key_pos = (device - (SUB - 1)) * length + jnp.arange(SUB * length, dtype=jnp.int32)
    visible = (
        (key_pos[None, :] <= query_pos[:, None])
        & (key_pos[None, :] >= 0)
        & (
            document_of(key_pos, doc_lengths)[None, :]
            == document_of(query_pos, doc_lengths)[:, None]
        )
    )
    query_split = soft_query.reshape(length, kv_local, group_size, DH)
    grad_split = soft_grad.reshape(length, kv_local, group_size, DH)
    key_win = window[0, :, 0:DH]
    value_win = window[1, :, 0:DH]
    query_heads = jnp.transpose(query_split[:, 0], (1, 0, 2))
    grad_heads = jnp.transpose(grad_split[:, 0], (1, 0, 2))
    grad_key, grad_value, grad_query = softmax_head(
        query_heads, grad_heads, key_win, value_win, visible
    )
    query_grads = [jnp.transpose(grad_query, (1, 0, 2))]
    soft_dq = jnp.stack(query_grads, axis=1).reshape(length, kv_local * group_size * DH)
    partial_value = jnp.stack([grad_key, grad_value])

    def block_of(offset):
        slot = SUB - 1 - offset
        return partial_value[:, slot * length : (slot + 1) * length]

    summed = block_of(0)
    for offset in range(1, SUB):
        summed = summed + passed_along(block_of(offset), "ctx", -offset)
    return (soft_dq, summed[0].astype(jnp.bfloat16), summed[1].astype(jnp.bfloat16))


def per_device(
    lin_query,
    lin_keys,
    lin_values,
    lin_grad,
    norm_gain,
    log_decay,
    state_in,
    soft_query,
    soft_keys,
    soft_values,
    soft_grad,
    projections,
    doc_lengths,
):
    soft_dq, soft_dk, soft_dv = softmax_part(
        soft_query, soft_keys, soft_values, soft_grad, doc_lengths
    )
    kv_grads = jnp.stack([soft_dk, soft_dv], axis=1)
    carried_back = lax.psum_scatter(
        jnp.einsum("crk,tck->rt", projections, kv_grads, preferred_element_type=jnp.float32),
        "head",
        scatter_dimension=0,
        tiled=True,
    )
    cotangent = lin_grad.astype(jnp.float32) + carried_back.T
    lin_dq, lin_dk, lin_dv = lightning_part(
        lin_query, lin_keys, lin_values, cotangent, norm_gain, log_decay, state_in
    )
    return (lin_dq, lin_dk, lin_dv, soft_dq, soft_dk, soft_dv)


def solution(mesh):
    in_specs = (
        P("ctx", "head"),
        P("ctx", "head"),
        P("ctx", "head"),
        P("ctx", "head"),
        P("head"),
        P("head", None),
        P("ctx", "head", None, None),
        P("ctx", "head"),
        P("ctx", "head"),
        P("ctx", "head"),
        P("ctx", "head"),
        P(None, None, "head"),
        P(),
    )
    out_specs = (
        P("ctx", "head"),
        P("ctx", "head"),
        P("ctx", "head"),
        P("ctx", "head"),
        P("ctx", "head"),
        P("ctx", "head"),
    )
    return jax.shard_map(
        per_device, mesh=mesh, in_specs=in_specs, out_specs=out_specs, check_vma=False
    )
```

profile of v0, /device:TPU:32, one launch (start us, length us, event | category | flops | bytes accessed | tf_op | source)
XLA Modules:
  0.0 368.0 jit_solution(18281954963981145327)
XLA Ops:
  8.3 3.8 %collective-permute-start.2 = (bf16[2,256,128]{2,1,0:T(8,128)(2,1)S(1)}, bf16[2,256,128]{2,1,0:T(8,128)(2,1)S(1)}, u32[]{:S(2)}, u32[]{:S(2)}) collective-permute-start(bf16[2,256,128]{2,1,0:T(8,128)(2,1)S(1)} %pad_maximum_fusion.1), channel_id=1, source_target_pairs={{0,8},{8,16},{16,24},{24,32},{32,40},{40,48},{48,56},{56,64},{64,7... | collective-permute-start | bytes 393224 | tf_op jit(solution)/shard_map/ppermute | solution.py:18
  12.1 7.0 %collective-permute-start.1 = (bf16[2,256,128]{2,1,0:T(8,128)(2,1)S(1)}, bf16[2,256,128]{2,1,0:T(8,128)(2,1)}, u32[]{:S(2)}, u32[]{:S(2)}) collective-permute-start(bf16[2,256,128]{2,1,0:T(8,128)(2,1)S(1)} %pad_maximum_fusion.1), channel_id=1, source_target_pairs={{0,16},{8,24},{16,32},{24,40},{32,48},{40,56},{48,64},{56,72},{64,... | collective-permute-start | bytes 393224 | tf_op jit(solution)/shard_map/ppermute | solution.py:18
  19.2 6.5 %collective-permute-start = (bf16[2,256,128]{2,1,0:T(8,128)(2,1)S(1)}, bf16[2,256,128]{2,1,0:T(8,128)(2,1)}, u32[]{:S(2)}, u32[]{:S(2)}) collective-permute-start(bf16[2,256,128]{2,1,0:T(8,128)(2,1)S(1)} %pad_maximum_fusion.1), channel_id=1, source_target_pairs={{0,24},{8,32},{16,40},{24,48},{32,56},{40,64},{48,72},{56,80},{64,... | collective-permute-start | bytes 393224 | tf_op jit(solution)/shard_map/ppermute | solution.py:18
  27.4 1.9 copy_bitcast_fusion.1
  33.8 39.3 %while.15 = (s32[]{:T(128)}, f32[1024,128]{1,0:T(8,128)}, f32[1024,128]{1,0:T(8,128)S(1)}, bf16[4,512,128]{2,1,0:T(8,128)(2,1)}, bf16[4,512,128]{2,1,0:T(8,128)(...) while((s32[]{:T(128)}, f32[1024,128]{1,0:T(8,128)}, ...), condition=%wide.region_7.8_spmd.clone, body=%wide.region_3.7_spmd.clone.sunk | while | flops 816052736 | bytes 27801824 | solution.py:153
  35.5 1.5 fusion.122
  45.4 1.5 fusion.122
  50.9 1.5 convolution_add_fusion.5
  55.2 1.5 fusion.122
  60.7 1.5 convolution_add_fusion.5
  65.0 1.5 fusion.122
  74.3 1.9 collective-permute-start.3
  78.8 10.3 %collective-permute-done.3 = f32[2,256,128]{2,1,0:T(8,128)S(1)} collective-permute-done((f32[2,256,128]{2,1,0:T(8,128)S(1)}, f32[2,256,128]{2,1,0:T(8,128)S(1)}, u32[]{:S(2)}, u32[]{:S(2)}) %collective-permute-start.3) | collective-permute-done | bytes 262176 | tf_op jit(solution)/shard_map/ppermute | solution.py:18
  89.1 19.3 %collective-permute-done.5 = f32[2,256,128]{2,1,0:T(8,128)S(1)} collective-permute-done((f32[2,256,128]{2,1,0:T(8,128)S(1)}, f32[2,256,128]{2,1,0:T(8,128)S(1)}, u32[]{:S(2)}, u32[]{:S(2)}) %collective-permute-start.5) | collective-permute-done | bytes 262176 | tf_op jit(solution)/shard_map/ppermute | solution.py:18
  108.5 4.6 %collective-permute-done.4 = f32[2,256,128]{2,1,0:T(8,128)S(1)} collective-permute-done((f32[2,256,128]{2,1,0:T(8,128)S(1)}, f32[2,256,128]{2,1,0:T(8,128)S(1)}, u32[]{:S(2)}, u32[]{:S(2)}) %collective-permute-start.4) | collective-permute-done | bytes 262176 | tf_op jit(solution)/shard_map/ppermute | solution.py:18
  113.8 2.7 convolution_bitcast_fusion
  122.3 42.6 %reduce-scatter.2.cloned.1.call-done = f32[512,256]{0,1:T(8,128)} async-done(((f32[4096,256]{0,1:T(8,128)}), f32[512,256]{0,1:T(8,128)}) %reduce-scatter.2.cloned.1.call-update) | async-done | bytes 524304 | tf_op jit(solution)/shard_map/reduce_scatter | solution.py:217
  164.9 1.9 bitcast_add_fusion
  168.1 2.2 fusion.36
  170.3 13.1 %all-reduce.1 = (f32[256]{0:T(256)S(1)}, f32[256]{0:T(256)S(1)}) all-reduce(f32[256]{0:T(256)S(1)} %get-tuple-element.158, f32[256]{0:T(256)S(1)} %get-tuple-element.157), channel_id=1, replica_groups=mesh['ctx'=64,'head'=8] {'head'}, use_global_device_ids=true, to_apply=%region_14.15 | all-reduce | flops 512 | bytes 4096 | tf_op jit(solution)/shard_map/psum | solution.py:56
  195.5 146.7 %all-gather.3.cloned.1.call-done = bf16[256,128,128]{2,1,0:T(8,128)(2,1)} async-done(((bf16[4,128,128]{2,1,0:T(8,128)(2,1)}), bf16[256,128,128]{2,1,0:T(8,128)(2,1)}) %all-gather.3.cloned.1.call-update) | async-done | bytes 8388624 | tf_op jit(solution)/shard_map/all_gather | solution.py:83
  342.2 12.2 %fusion.19 = bf16[4,1,128,128]{3,1,2,0:T(2,128)(2,1)} fusion(f32[4,64,1,1]{1,2,3,0:T(1,128)S(1)} %bitcast.267, bf16[64,4,128,128]{3,2,1,0:T(8,128)(2,1)} %bitcast.244), kind=kOutput, calls=%fused_computation.26 | convolution fusion | flops 50331648 | bytes 8520704 | tf_op jit(solution)/shard_map/hn,nhde->hde/dot_general | solution.py:90
  355.4 1.9 fusion.33
  357.3 1.8 copy.148
  (154 shorter events, 63.9 us)
Async XLA Ops:
  7.2 106.6 %copy-start = (bf16[2,4096,128]{2,1,0:T(8,128)(2,1)S(1)}, bf16[2,4096,128]{2,1,0:T(8,128)(2,1)}, u32[]{:S(2)}) copy-start(bf16[2,4096,128]{2,1,0:T(8,128)(2,1)} %param.26) | copy-start | bytes 6291460
  7.2 25.6 %copy-start.14 = (bf16[256,128]{1,0:T(8,128)(2,1)S(1)}, bf16[256,128]{1,0:T(8,128)(2,1)}, u32[]{:S(2)}) copy-start(bf16[256,128]{1,0:T(8,128)(2,1)} %param.24) | copy-start | bytes 196612
  7.2 25.6 %copy-start.15 = (bf16[256,128]{1,0:T(8,128)(2,1)S(1)}, bf16[256,128]{1,0:T(8,128)(2,1)}, u32[]{:S(2)}) copy-start(bf16[256,128]{1,0:T(8,128)(2,1)} %param.23) | copy-start | bytes 196612
  7.2 157.7 %reduce-scatter.2.cloned.1.call-start = ((), (), s32[]{:S(2)}) async-start(), calls=%async_computation.1 | async-start | bytes 4718592 | tf_op jit(solution)/shard_map/reduce_scatter | solution.py:217
  8.3 24.3 %collective-permute-start.2 = (bf16[2,256,128]{2,1,0:T(8,128)(2,1)S(1)}, bf16[2,256,128]{2,1,0:T(8,128)(2,1)S(1)}, u32[]{:S(2)}, u32[]{:S(2)}) collective-permute-start(bf16[2,256,128]{2,1,0:T(8,128)(2,1)S(1)} %pad_maximum_fusion.1), channel_id=1, source_target_pairs={{0,8},{8,16},{16,24},{24,32},{32,40},{40,48},{48,56},{56,64},{64,7... | collective-permute-start | bytes 393224 | tf_op jit(solution)/shard_map/ppermute | solution.py:18
  12.1 20.5 %collective-permute-start.1 = (bf16[2,256,128]{2,1,0:T(8,128)(2,1)S(1)}, bf16[2,256,128]{2,1,0:T(8,128)(2,1)}, u32[]{:S(2)}, u32[]{:S(2)}) collective-permute-start(bf16[2,256,128]{2,1,0:T(8,128)(2,1)S(1)} %pad_maximum_fusion.1), channel_id=1, source_target_pairs={{0,16},{8,24},{16,32},{24,40},{32,48},{40,56},{48,64},{56,72},{64,... | collective-permute-start | bytes 393224 | tf_op jit(solution)/shard_map/ppermute | solution.py:18
  19.2 13.6 %collective-permute-start = (bf16[2,256,128]{2,1,0:T(8,128)(2,1)S(1)}, bf16[2,256,128]{2,1,0:T(8,128)(2,1)}, u32[]{:S(2)}, u32[]{:S(2)}) collective-permute-start(bf16[2,256,128]{2,1,0:T(8,128)(2,1)S(1)} %pad_maximum_fusion.1), channel_id=1, source_target_pairs={{0,24},{8,32},{16,40},{24,48},{32,56},{40,64},{48,72},{56,80},{64,... | collective-permute-start | bytes 393224 | tf_op jit(solution)/shard_map/ppermute | solution.py:18
  42.5 1.1 copy-start.2
  52.4 1.1 copy-start.2
  62.2 1.1 copy-start.2
  72.0 1.1 copy-start.2
  73.1 39.9 %copy-start.3 = (f32[1024,128]{1,0:T(8,128)S(1)}, f32[1024,128]{1,0:T(8,128)}, u32[]{:S(2)}) copy-start(f32[1024,128]{1,0:T(8,128)} %get-tuple-element.55) | copy-start | bytes 1572868
  74.3 14.9 %collective-permute-start.3 = (f32[2,256,128]{2,1,0:T(8,128)S(1)}, f32[2,256,128]{2,1,0:T(8,128)S(1)}, u32[]{:S(2)}, u32[]{:S(2)}) collective-permute-start(f32[2,256,128]{2,1,0:T(8,128)S(1)} %get-tuple-element.181), channel_id=1, source_target_pairs={{8,0},{16,8},{24,16},{32,24},{40,32},{48,40},{56,48},{64,56},{72,6... | collective-permute-start | bytes 786440 | tf_op jit(solution)/shard_map/ppermute | solution.py:18
  76.2 32.3 %collective-permute-start.5 = (f32[2,256,128]{2,1,0:T(8,128)S(1)}, f32[2,256,128]{2,1,0:T(8,128)S(1)}, u32[]{:S(2)}, u32[]{:S(2)}) collective-permute-start(f32[2,256,128]{2,1,0:T(8,128)S(1)} %get-tuple-element.182), channel_id=1, source_target_pairs={{24,0},{32,8},{40,16},{48,24},{56,32},{64,40},{72,48},{80,56},{88,... | collective-permute-start | bytes 786440 | tf_op jit(solution)/shard_map/ppermute | solution.py:18
  77.5 35.5 %collective-permute-start.4 = (f32[2,256,128]{2,1,0:T(8,128)S(1)}, f32[2,256,128]{2,1,0:T(8,128)S(1)}, u32[]{:S(2)}, u32[]{:S(2)}) collective-permute-start(f32[2,256,128]{2,1,0:T(8,128)S(1)} %get-tuple-element.183), channel_id=1, source_target_pairs={{16,0},{24,8},{32,16},{40,24},{48,32},{56,40},{64,48},{72,56},{80,... | collective-permute-start | bytes 786440 | tf_op jit(solution)/shard_map/ppermute | solution.py:18
  116.4 2.6 copy-start.13
  116.5 3.4 copy-start.9
  116.5 4.7 %copy-start.10 = (bf16[256,512]{1,0:T(8,128)(2,1)S(1)}, bf16[256,512]{1,0:T(8,128)(2,1)}, u32[]{:S(2)}) copy-start(bf16[256,512]{1,0:T(8,128)(2,1)} %param.17) | copy-start | bytes 786436
  116.5 225.7 %all-gather.3.cloned.1.call-start = ((), (), s32[]{:S(2)}) async-start(), calls=%async_computation.2 | async-start | bytes 8519680 | tf_op jit(solution)/shard_map/all_gather | solution.py:83
  118.6 46.3 %copy-start.12 = (bf16[256,512]{1,0:T(8,128)(2,1)S(1)}, bf16[256,512]{1,0:T(8,128)(2,1)}, u32[]{:S(2)}) copy-start(bf16[256,512]{1,0:T(8,128)(2,1)} %param.18) | copy-start | bytes 786436
  121.2 46.9 %copy-start.11 = (bf16[1,4,128,128]{3,2,1,0:T(8,128)(2,1)S(1)}, bf16[1,4,128,128]{3,2,1,0:T(8,128)(2,1)}, u32[]{:S(2)}) copy-start(bf16[1,4,128,128]{3,2,1,0:T(8,128)(2,1)} %param.21) | copy-start | bytes 393220
  121.2 46.9 %copy-start.17 = (f32[512]{0:T(512)S(1)}, f32[512]{0:T(512)}, u32[]{:S(2)}) copy-start(f32[512]{0:T(512)} %param.19) | copy-start | bytes 6148
  189.4 3.7 %copy-start.6 = (bf16[4,256,256]{2,1,0:T(8,128)(2,1)S(1)}, bf16[4,256,256]{2,1,0:T(8,128)(2,1)}, u32[]{:S(2)}) copy-start(bf16[4,256,256]{2,1,0:T(8,128)(2,1)} %copy-done.5) | copy-start | bytes 1572868
  342.2 13.3 %copy-start.7 = (f32[256,4,128]{0,2,1:T(8,128)S(1)}, f32[256,4,128]{0,2,1:T(8,128)}, u32[]{:S(2)}) copy-start(f32[256,4,128]{0,2,1:T(8,128)} %convolution_bitcast_fusion.4) | copy-start | bytes 1572868
  (11 other events, 10.2 us)
Sparse Core Ops, SparseCore 0:
  116.6 48.2 reduce-scatter.1
  185.7 156.4 all-gather.2
where the time goes:
time: 369 us; the launch traced here: 368 us
  waiting for transfers between devices  224 us (61%)
  matrix products  49.9 us (14%)
  local copies, waits for them, and re-layouts  27.2 us (7%)
  starting transfers between devices  22 us (6%)
  other arithmetic  17.5 us (5%)
  between operations  14.3 us (4%)
  blocking collectives  13.1 us (4%)
    all_gather x1, waiting for transfers between devices, lightning_part(): block_in = lax.all_gather(summary[None], 'ctx', axis=0, tiled=True)  147 us
    reduce_scatter x1, waiting for transfers between devices, per_device(): lax.psum_scatter(jnp.einsum('crk,tck->rt', projections, kv_grads, preferr...  42.6 us
    ppermute x6, waiting for transfers between devices, passed_along(): return lax.ppermute(block, axis, route)  34.4 us
    ppermute x6, starting transfers between devices, passed_along(): return lax.ppermute(block, axis, route)  21.9 us
    psum x1, blocking collectives, lightning_part(): lax.psum((jnp.sum(lin_out * lin_out, axis=(1, 2)), jnp.sum(gated * lin_ou...  13.1 us
    dot_general x1, matrix products, lightning_part(): jnp.einsum('hn,nhde->hde', factors, block_in.astype(jnp.float32), precisi...  12.2 us
    unnamed x38, local copies, waits for them, and re-layouts  8.16 us
  transfers between devices with their start and end apart: 8, of which 6 were waited for; matrix products, arithmetic and copies ran while one was open for 6% of the time, Pallas kernels for 0%

commit v1 on v0

--- a/solution.py
+++ b/solution.py
@@ -80,7 +80,9 @@
         [jnp.zeros((head_count, 1), jnp.float32), jnp.cumsum(totals, axis=1)], axis=1
     )
     anchor = lax.dynamic_slice_in_dim(starts, device + 1, 1, 1)
-    block_in = lax.all_gather(summary[None], "ctx", axis=0, tiled=True)
+    block_in = jnp.concatenate(
+        lax.all_to_all(jnp.stack([summary[None]] * lax.axis_size("ctx")), "ctx", 0, 0), axis=0
+    )
     block_count = block_in.shape[0]
     block_index = jnp.arange(block_count, dtype=jnp.int32)
     log_level = lax.slice_in_dim(starts, 0, block_count, axis=1)

time: 369 us -> 617 us (1.67)
  waiting for transfers between devices: 224 us -> 436 us
  matrix products: 49.9 us -> 67.3 us
  starting transfers between devices: 22 us -> 37.3 us
  other arithmetic: 17.5 us -> 25.1 us
    all_to_all x0 -> x1, waiting for transfers between devices: none -> 358 us  [lightning_part(): lax.all_to_all(jnp.stack([summary[None]] * lax.axis_size('ctx')), 'ctx',...]
    all_gather x1 -> x0, waiting for transfers between devices: 147 us -> none  [lightning_part(): block_in = lax.all_gather(summary[None], 'ctx', axis=0, tiled=True)]
    all_to_all x0 -> x1, starting transfers between devices: none -> 16 us  [lightning_part(): lax.all_to_all(jnp.stack([summary[None]] * lax.axis_size('ctx')), 'ctx',...]
    dot_general x4, matrix products: 2.03 us -> 8.91 us  [one_turn(): output = jnp.dot(prob_low, value_win, preferred_element_type=jnp.float32)]
  transfers between devices with their start and end apart: 8 -> 8, of which waited for: 6 -> 6; matrix products, arithmetic and copies ran while one was open for 6% -> 3% of each run, Pallas kernels for 0% -> 0%
where the time goes in v1:
time: 617 us; the launch traced here: 615 us
  waiting for transfers between devices  436 us (71%)
  matrix products  67.3 us (11%)
  starting transfers between devices  37.3 us (6%)
  other arithmetic  25.1 us (4%)
  local copies, waits for them, and re-layouts  21.8 us (4%)
  between operations  14.4 us (2%)
  blocking collectives  13 us (2%)
    all_to_all x1, waiting for transfers between devices, lightning_part(): lax.all_to_all(jnp.stack([summary[None]] * lax.axis_size('ctx')), 'ctx',...  358 us
    reduce_scatter x1, waiting for transfers between devices, per_device(): lax.psum_scatter(jnp.einsum('crk,tck->rt', projections, kv_grads, preferr...  40.2 us
    ppermute x6, waiting for transfers between devices, passed_along(): return lax.ppermute(block, axis, route)  38.4 us
    ppermute x6, starting transfers between devices, passed_along(): return lax.ppermute(block, axis, route)  21.3 us
    all_to_all x1, starting transfers between devices, lightning_part(): lax.all_to_all(jnp.stack([summary[None]] * lax.axis_size('ctx')), 'ctx',...  16 us
    psum x1, blocking collectives, lightning_part(): lax.psum((jnp.sum(lin_out * lin_out, axis=(1, 2)), jnp.sum(gated * lin_ou...  13 us
  transfers between devices with their start and end apart: 8, of which 6 were waited for; matrix products, arithmetic and copies ran while one was open for 3% of the time, Pallas kernels for 0%

profile of v1, /device:TPU:32, one launch (start us, length us, event | category | flops | bytes accessed | tf_op | source)
XLA Modules:
  0.0 615.5 jit_solution(14931589498535866414)
XLA Ops:
  8.3 7.7 %collective-permute-start = (bf16[2,256,128]{2,1,0:T(8,128)(2,1)S(1)}, bf16[2,256,128]{2,1,0:T(8,128)(2,1)S(1)}, u32[]{:S(2)}, u32[]{:S(2)}) collective-permute-start(bf16[2,256,128]{2,1,0:T(8,128)(2,1)S(1)} %pad_maximum_fusion.1), channel_id=1, source_target_pairs={{0,24},{8,32},{16,40},{24,48},{32,56},{40,64},{48,72},{56,80},{64,... | collective-permute-start | bytes 393224 | tf_op jit(solution)/shard_map/ppermute | solution.py:18
  16.0 5.8 collective-permute-start.1
  21.9 3.2 collective-permute-start.2
  31.2 3.3 collective-permute-done.2
  35.6 60.0 %while.15 = (s32[]{:T(128)}, f32[1024,128]{1,0:T(8,128)}, f32[1024,128]{1,0:T(8,128)}, bf16[4,512,128]{2,1,0:T(8,128)(2,1)}, bf16[4,512,128]{2,1,0:T(8,128)(2,1)...) while((s32[]{:T(128)}, f32[1024,128]{1,0:T(8,128)}, ...), condition=%wide.region_7.8_spmd.clone, body=%wide.region_3.7_spmd.clone.sunk | while | flops 816052736 | bytes 48250204 | solution.py:155
  40.3 2.2 fusion.125
  43.9 2.3 convolution_add_fusion.5
  54.3 2.2 fusion.125
  57.9 2.5 convolution_add_fusion.5
  62.5 2.4 convolution_add_fusion.6
  73.3 2.5 convolution_add_fusion.5
  77.8 2.4 convolution_add_fusion.6
  88.6 2.5 convolution_add_fusion.5
  93.2 2.4 convolution_add_fusion.6
  101.4 10.9 %collective-permute-done.3 = f32[2,256,128]{2,1,0:T(8,128)S(1)} collective-permute-done((f32[2,256,128]{2,1,0:T(8,128)S(1)}, f32[2,256,128]{2,1,0:T(8,128)S(1)}, u32[]{:S(2)}, u32[]{:S(2)}) %collective-permute-start.3) | collective-permute-done | bytes 262176 | tf_op jit(solution)/shard_map/ppermute | solution.py:18
  112.4 3.4 collective-permute-done.4
  115.8 20.7 %collective-permute-done.5 = f32[2,256,128]{2,1,0:T(8,128)S(1)} collective-permute-done((f32[2,256,128]{2,1,0:T(8,128)S(1)}, f32[2,256,128]{2,1,0:T(8,128)S(1)}, u32[]{:S(2)}, u32[]{:S(2)}) %collective-permute-start.5) | collective-permute-done | bytes 262176 | tf_op jit(solution)/shard_map/ppermute | solution.py:18
  138.1 2.7 convolution_bitcast_fusion
  146.1 40.2 %reduce-scatter.2.cloned.1.call-done = f32[512,256]{0,1:T(8,128)} async-done(((f32[4096,256]{0,1:T(8,128)}), f32[512,256]{0,1:T(8,128)}) %reduce-scatter.2.cloned.1.call-update) | async-done | bytes 524304 | tf_op jit(solution)/shard_map/reduce_scatter | solution.py:219
  189.8 13.0 %all-reduce.1 = (f32[256]{0:T(256)S(1)}, f32[256]{0:T(256)S(1)}) all-reduce(f32[256]{0:T(256)S(1)} %get-tuple-element.143, f32[256]{0:T(256)S(1)} %get-tuple-element.142), channel_id=1, replica_groups=mesh['ctx'=64,'head'=8] {'head'}, use_global_device_ids=true, to_apply=%region_14.15 | all-reduce | flops 512 | bytes 4096 | tf_op jit(solution)/shard_map/psum | solution.py:56
  204.2 5.3 stack.33
  209.5 16.0 %all-to-all-start = ((bf16[64,1,4,128,128]{4,3,2,1,0:T(8,128)(2,1)}), bf16[64,1,4,128,128]{4,3,2,1,0:T(8,128)(2,1)}, u32[]{:S(2)}, u32[]{:S(2)}) async-start(bf16[64,1,4,128,128]{4,3,2,1,0:T(8,128)(2,1)} %stack.33), calls=%async_computation.1 | async-start | bytes 16777216 | tf_op jit(solution)/shard_map/all_to_all | solution.py:84
  235.2 357.6 %all-to-all-done = bf16[64,1,4,128,128]{4,3,2,1,0:T(8,128)(2,1)} async-done(((bf16[64,1,4,128,128]{4,3,2,1,0:T(8,128)(2,1)}), bf16[64,1,4,128,128]{4,3,2,1,0:T(8,128)(2,1)}, u32[]{:S(2)}, u32[]{:S(2)}) %all-to-all-start) | async-done | bytes 8388640 | tf_op jit(solution)/shard_map/all_to_all | solution.py:84
  592.8 11.5 %fusion.19 = bf16[4,1,128,128]{3,1,2,0:T(2,128)(2,1)S(1)} fusion(f32[4,64,1,1]{1,2,3,0:T(1,128)S(1)} %bitcast.264, bf16[64,4,128,128]{3,2,1,0:T(8,128)(2,1)} %bitcast.33), kind=kOutput, calls=%fused_computation.26 | convolution fusion | flops 50331648 | bytes 8520704 | tf_op jit(solution)/shard_map/hn,nhde->hde/dot_general | solution.py:92
  (202 shorter events, 77.7 us)
Async XLA Ops:
  7.2 131.0 %copy-start = (bf16[2,4096,128]{2,1,0:T(8,128)(2,1)S(1)}, bf16[2,4096,128]{2,1,0:T(8,128)(2,1)}, u32[]{:S(2)}) copy-start(bf16[2,4096,128]{2,1,0:T(8,128)(2,1)} %param.26) | copy-start | bytes 6291460
  7.2 27.4 %copy-start.22 = (bf16[256,128]{1,0:T(8,128)(2,1)S(1)}, bf16[256,128]{1,0:T(8,128)(2,1)}, u32[]{:S(2)}) copy-start(bf16[256,128]{1,0:T(8,128)(2,1)} %param.23) | copy-start | bytes 196612
  7.2 27.4 %copy-start.21 = (bf16[256,128]{1,0:T(8,128)(2,1)S(1)}, bf16[256,128]{1,0:T(8,128)(2,1)}, u32[]{:S(2)}) copy-start(bf16[256,128]{1,0:T(8,128)(2,1)} %param.24) | copy-start | bytes 196612
  7.2 179.0 %reduce-scatter.2.cloned.1.call-start = ((), (), s32[]{:S(2)}) async-start(), calls=%async_computation.2 | async-start | bytes 4718592 | tf_op jit(solution)/shard_map/reduce_scatter | solution.py:219
  8.3 22.9 %collective-permute-start = (bf16[2,256,128]{2,1,0:T(8,128)(2,1)S(1)}, bf16[2,256,128]{2,1,0:T(8,128)(2,1)S(1)}, u32[]{:S(2)}, u32[]{:S(2)}) collective-permute-start(bf16[2,256,128]{2,1,0:T(8,128)(2,1)S(1)} %pad_maximum_fusion.1), channel_id=1, source_target_pairs={{0,24},{8,32},{16,40},{24,48},{32,56},{40,64},{48,72},{56,80},{64,... | collective-permute-start | bytes 393224 | tf_op jit(solution)/shard_map/ppermute | solution.py:18
  16.0 15.2 %collective-permute-start.1 = (bf16[2,256,128]{2,1,0:T(8,128)(2,1)S(1)}, bf16[2,256,128]{2,1,0:T(8,128)(2,1)}, u32[]{:S(2)}, u32[]{:S(2)}) collective-permute-start(bf16[2,256,128]{2,1,0:T(8,128)(2,1)S(1)} %pad_maximum_fusion.1), channel_id=1, source_target_pairs={{0,16},{8,24},{16,32},{24,40},{32,48},{40,56},{48,64},{56,72},{64,... | collective-permute-start | bytes 393224 | tf_op jit(solution)/shard_map/ppermute | solution.py:18
  21.9 12.7 %collective-permute-start.2 = (bf16[2,256,128]{2,1,0:T(8,128)(2,1)S(1)}, bf16[2,256,128]{2,1,0:T(8,128)(2,1)}, u32[]{:S(2)}, u32[]{:S(2)}) collective-permute-start(bf16[2,256,128]{2,1,0:T(8,128)(2,1)S(1)} %pad_maximum_fusion.1), channel_id=1, source_target_pairs={{0,8},{8,16},{16,24},{24,32},{32,40},{40,48},{48,56},{56,64},{64,7... | collective-permute-start | bytes 393224 | tf_op jit(solution)/shard_map/ppermute | solution.py:18
  35.6 4.6 copy-start.3
  35.6 4.6 copy-start.5
  49.6 4.6 copy-start.3
  64.9 4.6 copy-start.3
  80.3 4.6 copy-start.3
  80.3 4.6 copy-start.5
  95.6 40.9 %copy-start.7 = (f32[1024,128]{1,0:T(8,128)S(1)}, f32[1024,128]{1,0:T(8,128)}, u32[]{:S(2)}) copy-start(f32[1024,128]{1,0:T(8,128)} %get-tuple-element.55) | copy-start | bytes 1572868
  96.9 15.5 %collective-permute-start.3 = (f32[2,256,128]{2,1,0:T(8,128)S(1)}, f32[2,256,128]{2,1,0:T(8,128)S(1)}, u32[]{:S(2)}, u32[]{:S(2)}) collective-permute-start(f32[2,256,128]{2,1,0:T(8,128)S(1)} %get-tuple-element.166), channel_id=1, source_target_pairs={{8,0},{16,8},{24,16},{32,24},{40,32},{48,40},{56,48},{64,56},{72,6... | collective-permute-start | bytes 786440 | tf_op jit(solution)/shard_map/ppermute | solution.py:18
  98.8 17.0 %collective-permute-start.4 = (f32[2,256,128]{2,1,0:T(8,128)S(1)}, f32[2,256,128]{2,1,0:T(8,128)S(1)}, u32[]{:S(2)}, u32[]{:S(2)}) collective-permute-start(f32[2,256,128]{2,1,0:T(8,128)S(1)} %get-tuple-element.168), channel_id=1, source_target_pairs={{16,0},{24,8},{32,16},{40,24},{48,32},{56,40},{64,48},{72,56},{80,... | collective-permute-start | bytes 786440 | tf_op jit(solution)/shard_map/ppermute | solution.py:18
  100.1 36.3 %collective-permute-start.5 = (f32[2,256,128]{2,1,0:T(8,128)S(1)}, f32[2,256,128]{2,1,0:T(8,128)S(1)}, u32[]{:S(2)}, u32[]{:S(2)}) collective-permute-start(f32[2,256,128]{2,1,0:T(8,128)S(1)} %get-tuple-element.167), channel_id=1, source_target_pairs={{24,0},{32,8},{40,16},{48,24},{56,32},{64,40},{72,48},{80,56},{88,... | collective-permute-start | bytes 786440 | tf_op jit(solution)/shard_map/ppermute | solution.py:18
  144.9 42.7 %copy-start.19 = (bf16[1,4,128,128]{3,2,1,0:T(8,128)(2,1)S(1)}, bf16[1,4,128,128]{3,2,1,0:T(8,128)(2,1)}, u32[]{:S(2)}) copy-start(bf16[1,4,128,128]{3,2,1,0:T(8,128)(2,1)} %param.21) | copy-start | bytes 393220
  144.9 42.7 %copy-start.26 = (f32[512]{0:T(512)S(1)}, f32[512]{0:T(512)}, u32[]{:S(2)}) copy-start(f32[512]{0:T(512)} %param.19) | copy-start | bytes 6148
  209.5 19.5 %copy-start.18 = (bf16[4,512,128]{2,1,0:T(8,128)(2,1)S(1)}, bf16[4,512,128]{2,1,0:T(8,128)(2,1)}, u32[]{:S(2)}) copy-start(bf16[4,512,128]{2,1,0:T(8,128)(2,1)} %get-tuple-element.57) | copy-start | bytes 1572868
  209.5 383.3 %all-to-all-start = ((bf16[64,1,4,128,128]{4,3,2,1,0:T(8,128)(2,1)}), bf16[64,1,4,128,128]{4,3,2,1,0:T(8,128)(2,1)}, u32[]{:S(2)}, u32[]{:S(2)}) async-start(bf16[64,1,4,128,128]{4,3,2,1,0:T(8,128)(2,1)} %stack.33), calls=%async_computation.1 | async-start | bytes 16777216 | tf_op jit(solution)/shard_map/all_to_all | solution.py:84
  225.5 4.7 copy-start.17
  231.8 361.0 %copy-start.25 = (f32[4,64]{1,0:T(4,128)S(1)}, f32[4,64]{1,0:T(4,128)}, u32[]{:S(2)}) copy-start(f32[4,64]{1,0:T(4,128)} %exponential_select_fusion.1) | copy-start | bytes 3076
  592.8 11.7 %copy-start.12 = (f32[256,4,128]{0,2,1:T(8,128)S(1)}, f32[256,4,128]{0,2,1:T(8,128)}, u32[]{:S(2)}) copy-start(f32[256,4,128]{0,2,1:T(8,128)} %convolution_bitcast_fusion.4) | copy-start | bytes 1572868
  (35 other events, 89.0 us)
Sparse Core Ops, SparseCore 0:
  141.0 45.2 reduce-scatter.1
